TPU v7x, 256 devices: a whole 4x4x8 slice. The times are simulated.
256 devices in a mesh: atom: 32 (over y, z_hi, core), sample: 8 (over z_lo, x).
Axes of the slice: x: 4, y: 4, z: 8 (z_hi: 4, z_lo: 2; z = z_hi * 2 + z_lo), core: 2. Of those that a mesh axis runs over, the one named last changes fastest.
Arguments:
- atom_act: bfloat16 [16, 8192, 128], P('sample', 'atom'), may hold values from -3 to 3
- atom_cond: bfloat16 [8192, 128], P('atom'), may hold values from -6 to 6
- ref_pos: float32 [3, 8192], P(None, 'atom'), may hold values from -9 to 9
- atom_token: int32 [8192], P('atom'), may hold values from 0 to 340, never falling along the last dimension, each value on 1 to 48 neighbouring positions
- w_pair_in: float32 [16, 5], replicated, may hold values from -2.5 to 2.5
- w_rel: float32 [16, 9], replicated, may hold values from -6 to 6
- w_cond_pair: bfloat16 [2, 128, 16], replicated, may hold values from -1 to 1
- w_pair_mlp: float32 [3, 16, 16], replicated, may hold values from -1.5 to 1.5
- w_bias: float32 [3, 4, 16], replicated, may hold values from -6 to 6
- w_cond: bfloat16 [3, 128, 768], replicated, may hold values from -0.5 to 0.5
- w_attn: bfloat16 [3, 128, 512], replicated, may hold values from -0.5 to 0.5
- q_bias: float32 [3, 128], replicated, may hold values from -48 to 48
- w_out: bfloat16 [3, 128, 128], replicated, may hold values from -1 to 1
- w_up: bfloat16 [3, 128, 512], replicated, may hold values from -0.5 to 0.5
- w_down: bfloat16 [3, 256, 128], replicated, may hold values from -0.375 to 0.375
Outputs:
- atom_out: bfloat16 [16, 8192, 128], P('sample', 'atom')
Inputs may be any that keep to these rules, and one draw needn't show every extreme that they name: `atom_token`: atoms of one token are consecutive and token numbers never fall along the atoms; a token has 1 to 48 atoms.
All inputs are finite; a program needn't handle non-finite values.
Results may differ from a plain program's by a relative error of at most 0.023.
The roundings to bfloat16 on the way count: a program that leaves them out, or rounds other values in their place, can miss the bound.
Values may be sent and summed in bfloat16 or wider, within the bound.
A program may use at most 64 MiB of HBM per device.

v0:
```python
import jax
import jax.numpy as jnp
from jax import lax
from jax.sharding import PartitionSpec as P

QW = 32
KW = 128
REL_CLIP = 4
NREL = 9


def with_halo(block, sides, width):
    for axis, dim in sides:
        count = lax.axis_size(axis)
        forward = [(i, i + 1) for i in range(count - 1)]
        backward = [(target, source) for source, target in forward]
        low = lax.ppermute(
            lax.slice_in_dim(block, block.shape[dim] - width, None, axis=dim), axis, forward
        )
        high = lax.ppermute(lax.slice_in_dim(block, 0, width, axis=dim), axis, backward)
        block = jnp.concatenate([low, block, high], axis=dim)
    return block


def layer_norm(values):
    average = jnp.mean(values, axis=-1, keepdims=True)
    centered = values - average
    variance = jnp.mean(centered * centered, axis=-1, keepdims=True)
    return centered * lax.rsqrt(variance + 1e-05)


def key_windows(padded, window_count, along):
    shifts = KW // QW
    new_shape = padded.shape[:along] + (window_count + shifts - 1, QW) + padded.shape[along + 1 :]
    blocks = padded.reshape(new_shape)
    pieces = [
        lax.slice_in_dim(blocks, start_at, start_at + window_count, axis=along)
        for start_at in range(shifts)
    ]
    stacked = jnp.stack(pieces, axis=along + 1)
    return stacked.reshape(padded.shape[:along] + (window_count, KW) + padded.shape[along + 1 :])


def pair_bias(query_feats, key_feats, key_valid, w_pair_in, w_rel, w_pair_mlp, w_bias):
    highest = lax.Precision.HIGHEST
    differences = query_feats[0:3][:, :, :, None] - key_feats[0:3][:, :, None, :]
    query_tok = query_feats[3][:, :, None]
    key_tok = key_feats[3][:, None, :]
    same_token = jnp.where((query_tok == key_tok) & key_valid[:, None, :], 1.0, 0.0).astype(
        jnp.float32
    )
    inverse = 1.0 / (1.0 + jnp.sum(differences * differences, axis=0))
    token_gap = jnp.clip(key_tok - query_tok, -REL_CLIP, REL_CLIP)
    classes = jnp.arange(NREL, dtype=jnp.float32) - REL_CLIP
    one_hot = jnp.where(token_gap[None] == classes[:, None, None, None], 1.0, 0.0).astype(
        jnp.float32
    )
    pair_rep = (
        jnp.einsum("cx,xwqk->cwqk", w_pair_in[:, 0:3], differences, precision=highest)
        * same_token[None]
    )
    pair_rep = pair_rep + w_pair_in[:, 3][:, None, None, None] * (inverse * same_token)[None]
    pair_rep = pair_rep + w_pair_in[:, 4][:, None, None, None] * same_token[None]
    pair_rep = pair_rep + jnp.einsum("cr,rwqk->cwqk", w_rel, one_hot, precision=highest)
    pair_rep = pair_rep + query_feats[4:][:, :, :, None] + key_feats[4:][:, :, None, :]
    hidden = jax.nn.relu(
        jnp.einsum("dc,cwqk->dwqk", w_pair_mlp[0], jax.nn.relu(pair_rep), precision=highest)
    )
    hidden = jax.nn.relu(jnp.einsum("dc,cwqk->dwqk", w_pair_mlp[1], hidden, precision=highest))
    pair_rep = pair_rep + jnp.einsum("dc,cwqk->dwqk", w_pair_mlp[2], hidden, precision=highest)
    average = jnp.mean(pair_rep, axis=0, keepdims=True)
    centered = pair_rep - average
    variance = jnp.mean(centered * centered, axis=0, keepdims=True)
    normed = centered * lax.rsqrt(jnp.maximum(variance, 0.1))
    return jnp.einsum("lhc,cwqk->lwhqk", w_bias, normed, precision=highest).astype(jnp.bfloat16)


def local(
    atom_act,
    atom_cond,
    ref_pos,
    atom_token,
    w_pair_in,
    w_rel,
    w_cond_pair,
    w_pair_mlp,
    w_bias,
    w_cond,
    w_attn,
    q_bias,
    w_out,
    w_up,
    w_down,
):
    samples, local_atoms, channels = atom_act.shape
    window_count = local_atoms // QW
    head_count = w_bias.shape[1]
    head_dim = channels // head_count
    halo_width = (KW - QW) // 2
    shifts = KW // QW
    hidden_units = w_down.shape[1]
    atom_rank = lax.axis_index("atom")
    total_atoms = local_atoms * lax.axis_size("atom")
    tokens = atom_token.astype(jnp.float32)
    active = jax.nn.relu(atom_cond)
    query_cond = jnp.einsum("ac,cp->pa", active, w_cond_pair[0], preferred_element_type=jnp.float32)
    key_cond = jnp.einsum("ac,cp->pa", active, w_cond_pair[1], preferred_element_type=jnp.float32)
    query_table = jnp.concatenate([ref_pos, tokens[None], query_cond], axis=0)
    key_table = jnp.concatenate([ref_pos, tokens[None], key_cond], axis=0)
    feature_rows = query_table.shape[0]
    key_padded = with_halo(key_table, (("atom", 1),), halo_width)
    position = (
        atom_rank * local_atoms
        - halo_width
        + jnp.arange(window_count)[:, None] * QW
        + jnp.arange(KW)[None, :]
    )
    key_valid = (position >= 0) & (position < total_atoms)
    query_windows = query_table.reshape(feature_rows, window_count, QW)
    share_count = window_count // lax.axis_size("sample")
    first_window = lax.axis_index("sample") * share_count
    my_queries = lax.dynamic_slice_in_dim(query_windows, first_window, share_count, 1)
    key_block = lax.dynamic_slice_in_dim(
        key_padded, first_window * QW, (share_count + shifts - 1) * QW, 1
    )
    my_keys = key_windows(key_block, share_count, 1)
    my_valid = lax.dynamic_slice_in_dim(key_valid, first_window, share_count, 0)
    my_bias = pair_bias(my_queries, my_keys, my_valid, w_pair_in, w_rel, w_pair_mlp, w_bias)
    attn_bias = lax.all_gather(my_bias, "sample", axis=1, tiled=True)
    scale_factor = head_dim ** (-0.5)
    residual = atom_act.astype(jnp.float32)
    for layer_index in range(w_attn.shape[0]):
        cond_values = jnp.dot(atom_cond, w_cond[layer_index], preferred_element_type=jnp.float32)
        modulated = (
            jax.nn.sigmoid(cond_values[:, 0:channels]) * layer_norm(residual)
            + cond_values[:, channels : 2 * channels]
        ).astype(jnp.bfloat16)
        weights = w_attn[layer_index]
        projected = jnp.einsum(
            "sac,cf->saf", modulated, weights, preferred_element_type=jnp.float32
        )
        queries = (projected[..., 0:channels] + q_bias[layer_index]).astype(jnp.bfloat16)
        gating = jax.nn.sigmoid(projected[..., 3 * channels : 4 * channels])
        keyval = projected[..., channels : 3 * channels].astype(jnp.bfloat16)
        keyval_padded = with_halo(keyval, (("atom", 1),), halo_width)
        keyval_windows = key_windows(keyval_padded, window_count, 1)
        query_heads = queries.reshape(samples, window_count, QW, head_count, head_dim)
        key_heads = keyval_windows[..., 0:channels].reshape(
            samples, window_count, KW, head_count, head_dim
        )
        value_heads = keyval_windows[..., channels : 2 * channels].reshape(
            samples, window_count, KW, head_count, head_dim
        )
        scores = (
            jnp.einsum(
                "swqhd,swkhd->swhqk", query_heads, key_heads, preferred_element_type=jnp.float32
            )
            * scale_factor
        )
        scores = scores + attn_bias[layer_index][None].astype(jnp.float32)
        scores = jnp.where(key_valid[None, :, None, None, :], scores, -jnp.inf)
        row_max = jnp.max(scores, axis=-1, keepdims=True)
        exponent = jnp.exp(scores - row_max)
        attn_probs = (exponent / jnp.sum(exponent, axis=-1, keepdims=True)).astype(jnp.bfloat16)
        mixed_out = jnp.einsum(
            "swhqk,swkhd->swqhd", attn_probs, value_heads, preferred_element_type=jnp.float32
        ).reshape(samples, local_atoms, channels)
        mixed_out = (mixed_out * gating).astype(jnp.bfloat16)
        attended = jnp.einsum(
            "sac,cd->sad", mixed_out, w_out[layer_index], preferred_element_type=jnp.float32
        )
        residual = residual + jax.nn.sigmoid(cond_values[:, 2 * channels : 3 * channels]) * attended
        modulated2 = (
            jax.nn.sigmoid(cond_values[:, 3 * channels : 4 * channels]) * layer_norm(residual)
            + cond_values[:, 4 * channels : 5 * channels]
        ).astype(jnp.bfloat16)
        up_values = jnp.einsum(
            "sac,cf->saf", modulated2, w_up[layer_index], preferred_element_type=jnp.float32
        )
        hidden = (
            jax.nn.silu(up_values[..., 0:hidden_units])
            * up_values[..., hidden_units : 2 * hidden_units]
        ).astype(jnp.bfloat16)
        transition = jnp.einsum(
            "saf,fc->sac", hidden, w_down[layer_index], preferred_element_type=jnp.float32
        )
        residual = (
            residual + jax.nn.sigmoid(cond_values[:, 5 * channels : 6 * channels]) * transition
        )
    return residual.astype(jnp.bfloat16)


def solution(mesh):
    in_specs = (
        P("sample", "atom", None),
        P("atom", None),
        P(None, "atom"),
        P("atom"),
        P(),
        P(),
        P(),
        P(),
        P(),
        P(),
        P(),
        P(),
        P(),
        P(),
        P(),
    )
    out_specs = P("sample", "atom", None)
    return jax.shard_map(local, mesh=mesh, in_specs=in_specs, out_specs=out_specs, check_vma=False)
```

profile of v0, /device:TPU:30, one launch (start us, length us, event | category | flops | bytes accessed | tf_op | source)
XLA Modules:
  0.0 158.6 jit_solution(17236440815866380441)
XLA Ops:
  3.4 1.2 fusion.242
  5.3 7.8 %collective-permute-start.1 = (bf16[2,48,256]{2,1,0:T(8,128)(2,1)}, bf16[2,48,256]{2,1,0:T(8,128)(2,1)}, u32[]{:S(2)}, u32[]{:S(2)}) collective-permute-start(bf16[2,48,256]{2,1,0:T(8,128)(2,1)} %get-tuple-element.37), channel_id=1, source_target_pairs={{8,0},{16,8},{24,16},{32,24},{40,32},{48,40},{56,48},{64,56},{72,6... | collective-permute-start | bytes 147464 | tf_op jit(solution)/shard_map/ppermute | solution.py:20
  13.1 1.9 %collective-permute-start = (bf16[2,48,256]{2,1,0:T(8,128)(2,1)}, bf16[2,48,256]{2,1,0:T(8,128)(2,1)}, u32[]{:S(2)}, u32[]{:S(2)}) collective-permute-start(bf16[2,48,256]{2,1,0:T(8,128)(2,1)} %get-tuple-element.36), channel_id=1, source_target_pairs={{0,8},{8,16},{16,24},{24,32},{32,40},{40,48},{48,56},{56,64},{64,7... | collective-permute-start | bytes 147464 | tf_op jit(solution)/shard_map/ppermute | solution.py:17
  16.4 1.9 %collective-permute-start.2 = (f32[20,48]{1,0:T(8,128)}, f32[20,48]{1,0:T(8,128)S(1)}, u32[]{:S(2)}, u32[]{:S(2)}) collective-permute-start(f32[20,48]{1,0:T(8,128)} %get-tuple-element.55), channel_id=1, source_target_pairs={{0,8},{8,16},{16,24},{24,32},{32,40},{40,48},{48,56},{56,64},{64,7... | collective-permute-start | bytes 11528 | tf_op jit(solution)/shard_map/ppermute | solution.py:17
  18.3 6.7 %collective-permute-start.3 = (f32[20,48]{1,0:T(8,128)}, f32[20,48]{1,0:T(8,128)}, u32[]{:S(2)}, u32[]{:S(2)}) collective-permute-start(f32[20,48]{1,0:T(8,128)} %get-tuple-element.54), channel_id=1, source_target_pairs={{8,0},{16,8},{24,16},{32,24},{40,32},{48,40},{56,48},{64,56},{72,6... | collective-permute-start | bytes 11528 | tf_op jit(solution)/shard_map/ppermute | solution.py:20
  29.6 1.3 slice_bitcast_fusion.23
  55.6 29.9 %all_gather.3 = bf16[3,8,4,32,128]{4,3,2,0,1:T(8,128)(2,1)S(1)} all-gather(bf16[3,1,4,32,128]{4,3,2,0,1:T(8,128)(2,1)S(1)} %copy.198), channel_id=1, replica_groups=mesh['atom'=32,'sample'=8] {'sample'}, dimensions={1}, use_global_device_ids=true | all-gather | bytes 884736 | tf_op jit(solution)/shard_map/all_gather | solution.py:129
  89.4 1.3 fusion.14
  91.7 4.6 %convolution_bitcast_fusion.2 = f32[2,8,32,4,32]{2,4,3,1,0:T(8,128)} fusion(bf16[2,8,128,4,32]{2,4,3,1,0:T(8,128)(2,1)S(1)} %bitcast.277, f32[2,8,4,32]{3,2,1,0:T(4,128)S(1)} %fusion.244, f32[2,8,4,32,128]{4,3,2,1,0:T(8,128)S(1)} %fusion.14), kind=kOutput, calls=%fused_computation.17 | convolution fusion | flops 17565824 | bytes 1843200 | tf_op jit(solution)/shard_map/swhqk,swkhd->swqhd/dot_general | solution.py:165
  96.4 1.6 %copy.199 = f32[2,8,32,4,32]{4,3,2,1,0:T(4,128)S(1)} copy(f32[2,8,32,4,32]{2,4,3,1,0:T(8,128)} %convolution_bitcast_fusion.2) | data formatting | bytes 524288 | tf_op jit(solution)/shard_map/swhqk,swkhd->swqhd/transpose | solution.py:165
  101.1 1.3 fusion.89
  104.5 1.2 fusion.247
  105.8 1.9 %collective-permute-start.5 = (bf16[2,48,256]{2,1,0:T(8,128)(2,1)S(1)}, bf16[2,48,256]{2,1,0:T(8,128)(2,1)S(1)}, u32[]{:S(2)}, u32[]{:S(2)}) collective-permute-start(bf16[2,48,256]{2,1,0:T(8,128)(2,1)S(1)} %get-tuple-element.35), channel_id=1, source_target_pairs={{8,0},{16,8},{24,16},{32,24},{40,32},{48,40},{56,48},{64,56},{72,6... | collective-permute-start | bytes 147464 | tf_op jit(solution)/shard_map/ppermute | solution.py:20
  107.7 2.6 %collective-permute-start.4 = (bf16[2,48,256]{2,1,0:T(8,128)(2,1)S(1)}, bf16[2,48,256]{2,1,0:T(8,128)(2,1)S(1)}, u32[]{:S(2)}, u32[]{:S(2)}) collective-permute-start(bf16[2,48,256]{2,1,0:T(8,128)(2,1)S(1)} %get-tuple-element.34), channel_id=1, source_target_pairs={{0,8},{8,16},{16,24},{24,32},{32,40},{40,48},{48,56},{56,64},{64,7... | collective-permute-start | bytes 147464 | tf_op jit(solution)/shard_map/ppermute | solution.py:17
  111.2 5.0 %collective-permute-done.4 = bf16[2,48,256]{2,1,0:T(8,128)(2,1)S(1)} collective-permute-done((bf16[2,48,256]{2,1,0:T(8,128)(2,1)S(1)}, bf16[2,48,256]{2,1,0:T(8,128)(2,1)S(1)}, u32[]{:S(2)}, u32[]{:S(2)}) %collective-permute-start.4) | collective-permute-done | bytes 49184 | tf_op jit(solution)/shard_map/ppermute | solution.py:17
  119.5 4.6 %convolution_bitcast_fusion.1 = f32[2,8,32,4,32]{2,4,3,1,0:T(8,128)} fusion(bf16[2,8,128,4,32]{2,4,3,1,0:T(8,128)(2,1)S(1)} %bitcast.278, f32[2,8,4,32]{3,2,1,0:T(4,128)S(1)} %fusion.248, f32[2,8,4,32,128]{4,3,2,1,0:T(8,128)S(1)} %fusion.12), kind=kOutput, calls=%fused_computation.13 | convolution fusion | flops 17565824 | bytes 1843200 | tf_op jit(solution)/shard_map/swhqk,swkhd->swqhd/dot_general | solution.py:165
  124.1 1.6 %copy.216 = f32[2,8,32,4,32]{4,3,2,1,0:T(4,128)S(1)} copy(f32[2,8,32,4,32]{2,4,3,1,0:T(8,128)} %convolution_bitcast_fusion.1) | data formatting | bytes 524288 | tf_op jit(solution)/shard_map/swhqk,swkhd->swqhd/transpose | solution.py:165
  128.8 1.3 fusion.91
  133.5 1.9 %collective-permute-start.7 = (bf16[2,48,256]{2,1,0:T(8,128)(2,1)S(1)}, bf16[2,48,256]{2,1,0:T(8,128)(2,1)S(1)}, u32[]{:S(2)}, u32[]{:S(2)}) collective-permute-start(bf16[2,48,256]{2,1,0:T(8,128)(2,1)S(1)} %get-tuple-element.33), channel_id=1, source_target_pairs={{8,0},{16,8},{24,16},{32,24},{40,32},{48,40},{56,48},{64,56},{72,6... | collective-permute-start | bytes 147464 | tf_op jit(solution)/shard_map/ppermute | solution.py:20
  135.5 2.4 %collective-permute-start.6 = (bf16[2,48,256]{2,1,0:T(8,128)(2,1)S(1)}, bf16[2,48,256]{2,1,0:T(8,128)(2,1)S(1)}, u32[]{:S(2)}, u32[]{:S(2)}) collective-permute-start(bf16[2,48,256]{2,1,0:T(8,128)(2,1)S(1)} %get-tuple-element.32), channel_id=1, source_target_pairs={{0,8},{8,16},{16,24},{24,32},{32,40},{40,48},{48,56},{56,64},{64,7... | collective-permute-start | bytes 147464 | tf_op jit(solution)/shard_map/ppermute | solution.py:17
  138.8 5.1 %collective-permute-done.6 = bf16[2,48,256]{2,1,0:T(8,128)(2,1)S(1)} collective-permute-done((bf16[2,48,256]{2,1,0:T(8,128)(2,1)S(1)}, bf16[2,48,256]{2,1,0:T(8,128)(2,1)S(1)}, u32[]{:S(2)}, u32[]{:S(2)}) %collective-permute-start.6) | collective-permute-done | bytes 49184 | tf_op jit(solution)/shard_map/ppermute | solution.py:17
  146.0 4.6 %convolution_bitcast_fusion = f32[2,8,32,4,32]{2,4,3,1,0:T(8,128)} fusion(bf16[2,8,128,4,32]{2,4,3,1,0:T(8,128)(2,1)S(1)} %bitcast.276, f32[2,8,4,32]{3,2,1,0:T(4,128)S(1)} %fusion.252, f32[2,8,4,32,128]{4,3,2,1,0:T(8,128)S(1)} %fusion.10), kind=kOutput, calls=%fused_computation.9 | convolution fusion | flops 17565824 | bytes 1843200 | tf_op jit(solution)/shard_map/swhqk,swkhd->swqhd/dot_general | solution.py:165
  150.6 1.6 %copy.233 = f32[2,8,32,4,32]{4,3,2,1,0:T(4,128)S(1)} copy(f32[2,8,32,4,32]{2,4,3,1,0:T(8,128)} %convolution_bitcast_fusion) | data formatting | bytes 524288 | tf_op jit(solution)/shard_map/swhqk,swkhd->swqhd/transpose | solution.py:165
  155.4 1.3 fusion.93
  (238 shorter events, 62.8 us)
Async XLA Ops:
  0.0 51.9 %copy-start = (f32[16,9]{1,0:T(8,128)S(1)}, f32[16,9]{1,0:T(8,128)}, u32[]{:S(2)}) copy-start(f32[16,9]{1,0:T(8,128)} %param.20) | copy-start | bytes 1732
  0.0 1.0 copy-start.1
  4.6 28.0 %copy-start.2 = (f32[2,256,512]{2,1,0:T(8,128)}, f32[2,256,512]{2,1,0:T(8,128)S(1)}, u32[]{:S(2)}) copy-start(f32[2,256,512]{2,1,0:T(8,128)S(1)} %get-tuple-element.65) | copy-start | bytes 3145732
  4.6 10.4 %copy-start.37 = (bf16[2,128,16]{1,2,0:T(8,128)(2,1)S(1)}, bf16[2,128,16]{1,2,0:T(8,128)(2,1)}, u32[]{:S(2)}) copy-start(bf16[2,128,16]{1,2,0:T(8,128)(2,1)} %param.21) | copy-start | bytes 24580
  5.3 81.3 %collective-permute-start.1 = (bf16[2,48,256]{2,1,0:T(8,128)(2,1)}, bf16[2,48,256]{2,1,0:T(8,128)(2,1)}, u32[]{:S(2)}, u32[]{:S(2)}) collective-permute-start(bf16[2,48,256]{2,1,0:T(8,128)(2,1)} %get-tuple-element.37), channel_id=1, source_target_pairs={{8,0},{16,8},{24,16},{32,24},{40,32},{48,40},{56,48},{64,56},{72,6... | collective-permute-start | bytes 147464 | tf_op jit(solution)/shard_map/ppermute | solution.py:20
  13.1 2.1 %copy-start.43 = (s32[256]{0:T(256)S(1)}, s32[256]{0:T(256)}, u32[]{:S(2)}) copy-start(s32[256]{0:T(256)} %param.18) | copy-start | bytes 3076
  13.1 73.5 %collective-permute-start = (bf16[2,48,256]{2,1,0:T(8,128)(2,1)}, bf16[2,48,256]{2,1,0:T(8,128)(2,1)}, u32[]{:S(2)}, u32[]{:S(2)}) collective-permute-start(bf16[2,48,256]{2,1,0:T(8,128)(2,1)} %get-tuple-element.36), channel_id=1, source_target_pairs={{0,8},{8,16},{16,24},{24,32},{32,40},{40,48},{48,56},{56,64},{64,7... | collective-permute-start | bytes 147464 | tf_op jit(solution)/shard_map/ppermute | solution.py:17
  16.4 32.2 %collective-permute-start.2 = (f32[20,48]{1,0:T(8,128)}, f32[20,48]{1,0:T(8,128)S(1)}, u32[]{:S(2)}, u32[]{:S(2)}) collective-permute-start(f32[20,48]{1,0:T(8,128)} %get-tuple-element.55), channel_id=1, source_target_pairs={{0,8},{8,16},{16,24},{24,32},{32,40},{40,48},{48,56},{56,64},{64,7... | collective-permute-start | bytes 11528 | tf_op jit(solution)/shard_map/ppermute | solution.py:17
  18.3 30.3 %collective-permute-start.3 = (f32[20,48]{1,0:T(8,128)}, f32[20,48]{1,0:T(8,128)}, u32[]{:S(2)}, u32[]{:S(2)}) collective-permute-start(f32[20,48]{1,0:T(8,128)} %get-tuple-element.54), channel_id=1, source_target_pairs={{8,0},{16,8},{24,16},{32,24},{40,32},{48,40},{56,48},{64,56},{72,6... | collective-permute-start | bytes 11528 | tf_op jit(solution)/shard_map/ppermute | solution.py:20
  27.0 1.2 copy-start.42
  29.0 4.4 %copy-start.34 = (f32[20,1,32]{2,1,0:T(1,128)}, f32[20,1,32]{2,1,0:T(1,128)S(1)}, u32[]{:S(2)}) copy-start(f32[20,1,32]{2,1,0:T(1,128)S(1)} %fusion.202) | copy-start | bytes 7684
  33.4 1.7 %copy-start.11 = (f32[256,128]{1,0:T(8,128)S(1)}, f32[256,128]{1,0:T(8,128)}, u32[]{:S(2)}) copy-start(f32[256,128]{1,0:T(8,128)} %get-tuple-element.31) | copy-start | bytes 393220
  90.7 1.0 copy-start.20
  100.1 1.0 copy-start.27
  101.1 1.3 copy-start.32
  105.8 5.2 %copy-start.4 = (f32[2,256,512]{2,1,0:T(8,128)}, f32[2,256,512]{2,1,0:T(8,128)S(1)}, u32[]{:S(2)}) copy-start(f32[2,256,512]{2,1,0:T(8,128)S(1)} %get-tuple-element.73) | copy-start | bytes 3145732
  105.8 5.4 %collective-permute-start.5 = (bf16[2,48,256]{2,1,0:T(8,128)(2,1)S(1)}, bf16[2,48,256]{2,1,0:T(8,128)(2,1)S(1)}, u32[]{:S(2)}, u32[]{:S(2)}) collective-permute-start(bf16[2,48,256]{2,1,0:T(8,128)(2,1)S(1)} %get-tuple-element.35), channel_id=1, source_target_pairs={{8,0},{16,8},{24,16},{32,24},{40,32},{48,40},{56,48},{64,56},{72,6... | collective-permute-start | bytes 147464 | tf_op jit(solution)/shard_map/ppermute | solution.py:20
  107.7 8.5 %collective-permute-start.4 = (bf16[2,48,256]{2,1,0:T(8,128)(2,1)S(1)}, bf16[2,48,256]{2,1,0:T(8,128)(2,1)S(1)}, u32[]{:S(2)}, u32[]{:S(2)}) collective-permute-start(bf16[2,48,256]{2,1,0:T(8,128)(2,1)S(1)} %get-tuple-element.34), channel_id=1, source_target_pairs={{0,8},{8,16},{16,24},{24,32},{32,40},{40,48},{48,56},{56,64},{64,7... | collective-permute-start | bytes 147464 | tf_op jit(solution)/shard_map/ppermute | solution.py:17
  118.5 1.0 copy-start.21
  128.8 1.3 copy-start.30
  133.5 5.0 %copy-start.3 = (f32[2,256,512]{2,1,0:T(8,128)}, f32[2,256,512]{2,1,0:T(8,128)S(1)}, u32[]{:S(2)}) copy-start(f32[2,256,512]{2,1,0:T(8,128)S(1)} %get-tuple-element.79) | copy-start | bytes 3145732
  133.5 5.3 %collective-permute-start.7 = (bf16[2,48,256]{2,1,0:T(8,128)(2,1)S(1)}, bf16[2,48,256]{2,1,0:T(8,128)(2,1)S(1)}, u32[]{:S(2)}, u32[]{:S(2)}) collective-permute-start(bf16[2,48,256]{2,1,0:T(8,128)(2,1)S(1)} %get-tuple-element.33), channel_id=1, source_target_pairs={{8,0},{16,8},{24,16},{32,24},{40,32},{48,40},{56,48},{64,56},{72,6... | collective-permute-start | bytes 147464 | tf_op jit(solution)/shard_map/ppermute | solution.py:20
  135.5 8.4 %collective-permute-start.6 = (bf16[2,48,256]{2,1,0:T(8,128)(2,1)S(1)}, bf16[2,48,256]{2,1,0:T(8,128)(2,1)S(1)}, u32[]{:S(2)}, u32[]{:S(2)}) collective-permute-start(bf16[2,48,256]{2,1,0:T(8,128)(2,1)S(1)} %get-tuple-element.32), channel_id=1, source_target_pairs={{0,8},{8,16},{16,24},{24,32},{32,40},{40,48},{48,56},{56,64},{64,7... | collective-permute-start | bytes 147464 | tf_op jit(solution)/shard_map/ppermute | solution.py:17
  155.4 1.3 copy-start.28
  (35 other events, 28.8 us)
where the time goes:
time: 160 us; the launch traced here: 159 us
  local copies, waits for them, and re-layouts  44.7 us (28%)
  matrix products  36.6 us (23%)
  blocking collectives  29.9 us (19%)
  starting transfers between devices  27.1 us (17%)
  waiting for transfers between devices  10.1 us (6%)
  other arithmetic  9.14 us (6%)
    all_gather x1, blocking collectives, local(): attn_bias = lax.all_gather(my_bias, 'sample', axis=1, tiled=True)  29.9 us
    ppermute x4, starting transfers between devices, with_halo(): lax.ppermute(lax.slice_in_dim(block, 0, width, axis=dim), axis, backward)  18.3 us
    unnamed x100, local copies, waits for them, and re-layouts  14.4 us
    dot_general x3, matrix products, local(): jnp.einsum('swhqk,swkhd->swqhd', attn_probs, value_heads, preferred_eleme...  13.9 us
    ppermute x4, waiting for transfers between devices, with_halo(): lax.ppermute(lax.slice_in_dim(block, block.shape[dim] - width, None, axis...  10 us
    ppermute x4, starting transfers between devices, with_halo(): lax.ppermute(lax.slice_in_dim(block, block.shape[dim] - width, None, axis...  8.82 us
    div x12, local copies, waits for them, and re-layouts, local(): jax.nn.sigmoid(cond_values[:, 0:channels]) * layer_norm(residual)  8.4 us
    transpose x3, local copies, waits for them, and re-layouts, local(): jnp.einsum('swhqk,swkhd->swqhd', attn_probs, value_heads, preferred_eleme...  4.88 us
  transfers between devices with their start and end apart: 8, of which 2 were waited for; matrix products, arithmetic and copies ran while one was open for 17% of the time, Pallas kernels for 0%

commit v1 on v0

--- a/solution.py
+++ b/solution.py
@@ -126,7 +126,9 @@
     my_keys = key_windows(key_block, share_count, 1)
     my_valid = lax.dynamic_slice_in_dim(key_valid, first_window, share_count, 0)
     my_bias = pair_bias(my_queries, my_keys, my_valid, w_pair_in, w_rel, w_pair_mlp, w_bias)
-    attn_bias = lax.all_gather(my_bias, "sample", axis=1, tiled=True)
+    attn_bias = jnp.concatenate(
+        lax.all_to_all(jnp.stack([my_bias] * lax.axis_size("sample")), "sample", 0, 0), axis=1
+    )
     scale_factor = head_dim ** (-0.5)
     residual = atom_act.astype(jnp.float32)
     for layer_index in range(w_attn.shape[0]):

time: 160 us -> 128 us (0.80)
  blocking collectives: 29.9 us -> 0 us
  starting transfers between devices: 27.1 us -> 33.6 us
  matrix products: 36.6 us -> 31.7 us
  local copies, waits for them, and re-layouts: 44.7 us -> 39.9 us
    all_gather x1 -> x0, blocking collectives: 29.9 us -> none  [local(): attn_bias = lax.all_gather(my_bias, 'sample', axis=1, tiled=True)]
    all_to_all x0 -> x1, starting transfers between devices: none -> 5.36 us  [local(): lax.all_to_all(jnp.stack([my_bias] * lax.axis_size('sample')), 'sample',...]
    transpose x3, local copies, waits for them, and re-layouts: 4.88 us -> 1.24 us  [local(): jnp.einsum('swhqk,swkhd->swqhd', attn_probs, value_heads, preferred_eleme...]
    dot_general x3, matrix products: 13.9 us -> 10.9 us  [local(): jnp.einsum('swhqk,swkhd->swqhd', attn_probs, value_heads, preferred_eleme...]
    dot_general x3, matrix products: 3.51 us -> 1.64 us  [local(): jnp.dot(atom_cond, w_cond[layer_index], preferred_element_type=jnp.float32)]
    unnamed x100 -> x96, local copies, waits for them, and re-layouts: 14.4 us -> 13.9 us
  transfers between devices with their start and end apart: 8 -> 9, of which waited for: 2 -> 2; matrix products, arithmetic and copies ran while one was open for 17% -> 20% of each run, Pallas kernels for 0% -> 0%
where the time goes in v1:
time: 128 us; the launch traced here: 126 us
  local copies, waits for them, and re-layouts  39.9 us (31%)
  starting transfers between devices  33.6 us (26%)
  matrix products  31.7 us (25%)
  waiting for transfers between devices  11.1 us (9%)
  other arithmetic  8.79 us (7%)
    ppermute x4, starting transfers between devices, with_halo(): lax.ppermute(lax.slice_in_dim(block, 0, width, axis=dim), axis, backward)  19.9 us
    unnamed x96, local copies, waits for them, and re-layouts  13.9 us
    ppermute x4, waiting for transfers between devices, with_halo(): lax.ppermute(lax.slice_in_dim(block, block.shape[dim] - width, None, axis...  11.1 us
    dot_general x3, matrix products, local(): jnp.einsum('swhqk,swkhd->swqhd', attn_probs, value_heads, preferred_eleme...  10.9 us
    div x12, local copies, waits for them, and re-layouts, local(): jax.nn.sigmoid(cond_values[:, 0:channels]) * layer_norm(residual)  8.36 us
    ppermute x4, starting transfers between devices, with_halo(): lax.ppermute(lax.slice_in_dim(block, block.shape[dim] - width, None, axis...  8.34 us
    all_to_all x1, starting transfers between devices, local(): lax.all_to_all(jnp.stack([my_bias] * lax.axis_size('sample')), 'sample',...  5.36 us
    dot_general x3, matrix products, local(): jnp.einsum('sac,cf->saf', modulated, weights, preferred_element_type=jnp....  4.73 us
  transfers between devices with their start and end apart: 9, of which 2 were waited for; matrix products, arithmetic and copies ran while one was open for 20% of the time, Pallas kernels for 0%

profile of v1, /device:TPU:30, one launch (start us, length us, event | category | flops | bytes accessed | tf_op | source)
XLA Modules:
  0.0 126.1 jit_solution(5404360250939047675)
XLA Ops:
  1.1 1.2 fusion.81
  3.4 2.3 %fusion.242 = (bf16[2,256,512]{2,1,0:T(8,128)(2,1)S(1)}, f32[2,256,512]{2,1,0:T(8,128)}) fusion(bf16[3,128,512]{2,1,0:T(8,128)(2,1)} %param.25, bf16[2,256,128]{1,2,0:T(8,128)(2,1)S(1)} %copy.178, f32[256,128]{0,1:T(8,128)S(1)} %copy.181, f32[2,256]{1,0:T(2,128)S(1)} %add_rsqrt_fusion.5, f32[2,256]{1,0:T(2,128)S(1)} %broadcast_multiply_fusion.6, ...), kind=kOutput, calls=%fused_computation.360 | convolution fusion | flops 67764224 | bytes 2101248 | tf_op jit(solution)/shard_map/sac,cf->saf/dot_general | solution.py:141
  6.3 7.8 %collective-permute-start.1 = (bf16[2,48,256]{2,1,0:T(8,128)(2,1)}, bf16[2,48,256]{2,1,0:T(8,128)(2,1)S(1)}, u32[]{:S(2)}, u32[]{:S(2)}) collective-permute-start(bf16[2,48,256]{2,1,0:T(8,128)(2,1)} %get-tuple-element.37), channel_id=1, source_target_pairs={{8,0},{16,8},{24,16},{32,24},{40,32},{48,40},{56,48},{64,56},{72,6... | collective-permute-start | bytes 147464 | tf_op jit(solution)/shard_map/ppermute | solution.py:20
  14.1 1.9 %collective-permute-start = (bf16[2,48,256]{2,1,0:T(8,128)(2,1)}, bf16[2,48,256]{2,1,0:T(8,128)(2,1)}, u32[]{:S(2)}, u32[]{:S(2)}) collective-permute-start(bf16[2,48,256]{2,1,0:T(8,128)(2,1)} %get-tuple-element.36), channel_id=1, source_target_pairs={{0,8},{8,16},{16,24},{24,32},{32,40},{40,48},{48,56},{56,64},{64,7... | collective-permute-start | bytes 147464 | tf_op jit(solution)/shard_map/ppermute | solution.py:17
  16.9 1.9 %collective-permute-start.2 = (f32[20,48]{1,0:T(8,128)S(1)}, f32[20,48]{1,0:T(8,128)S(1)}, u32[]{:S(2)}, u32[]{:S(2)}) collective-permute-start(f32[20,48]{1,0:T(8,128)S(1)} %get-tuple-element.55), channel_id=1, source_target_pairs={{0,8},{8,16},{16,24},{24,32},{32,40},{40,48},{48,56},{56,64},{64,7... | collective-permute-start | bytes 11528 | tf_op jit(solution)/shard_map/ppermute | solution.py:17
  18.8 6.7 %collective-permute-start.3 = (f32[20,48]{1,0:T(8,128)S(1)}, f32[20,48]{1,0:T(8,128)S(1)}, u32[]{:S(2)}, u32[]{:S(2)}) collective-permute-start(f32[20,48]{1,0:T(8,128)S(1)} %get-tuple-element.54), channel_id=1, source_target_pairs={{8,0},{16,8},{24,16},{32,24},{40,32},{48,40},{56,48},{64,56},{72,6... | collective-permute-start | bytes 11528 | tf_op jit(solution)/shard_map/ppermute | solution.py:20
  34.8 5.4 %all-to-all-start = ((bf16[8,3,1,4,32,128]{5,4,3,2,1,0:T(8,128)(2,1)}), bf16[8,3,1,4,32,128]{5,4,3,2,1,0:T(8,128)(2,1)S(1)}, u32[]{:S(2)}, u32[]{:S(2)}) async-start(bf16[8,3,1,4,32,128]{5,4,3,2,1,0:T(8,128)(2,1)} %stack.81), calls=%async_computation | async-start | bytes 1572864 | tf_op jit(solution)/shard_map/all_to_all | solution.py:130
  62.4 3.6 %convolution_bitcast_fusion.2 = f32[2,8,32,4,32]{2,4,3,1,0:T(8,128)S(1)} fusion(bf16[2,8,128,4,32]{2,4,3,1,0:T(8,128)(2,1)S(1)} %bitcast.280, f32[2,8,4,32]{3,2,1,0:T(4,128)S(1)} %fusion.244, f32[2,8,4,32,128]{4,3,2,1,0:T(8,128)S(1)} %fusion.14), kind=kOutput, calls=%fused_computation.17 | convolution fusion | flops 17565824 | bytes 1843200 | tf_op jit(solution)/shard_map/swhqk,swkhd->swqhd/dot_general | solution.py:167
  67.3 1.2 fusion.245
  69.5 1.3 fusion.89
  73.0 1.2 fusion.247
  74.2 3.5 %collective-permute-start.5 = (bf16[2,48,256]{2,1,0:T(8,128)(2,1)S(1)}, bf16[2,48,256]{2,1,0:T(8,128)(2,1)S(1)}, u32[]{:S(2)}, u32[]{:S(2)}) collective-permute-start(bf16[2,48,256]{2,1,0:T(8,128)(2,1)S(1)} %get-tuple-element.35), channel_id=1, source_target_pairs={{8,0},{16,8},{24,16},{32,24},{40,32},{48,40},{56,48},{64,56},{72,6... | collective-permute-start | bytes 147464 | tf_op jit(solution)/shard_map/ppermute | solution.py:20
  77.7 2.1 %collective-permute-start.4 = (bf16[2,48,256]{2,1,0:T(8,128)(2,1)S(1)}, bf16[2,48,256]{2,1,0:T(8,128)(2,1)S(1)}, u32[]{:S(2)}, u32[]{:S(2)}) collective-permute-start(bf16[2,48,256]{2,1,0:T(8,128)(2,1)S(1)} %get-tuple-element.34), channel_id=1, source_target_pairs={{0,8},{8,16},{16,24},{24,32},{32,40},{40,48},{48,56},{56,64},{64,7... | collective-permute-start | bytes 147464 | tf_op jit(solution)/shard_map/ppermute | solution.py:17
  80.8 5.4 %collective-permute-done.4 = bf16[2,48,256]{2,1,0:T(8,128)(2,1)S(1)} collective-permute-done((bf16[2,48,256]{2,1,0:T(8,128)(2,1)S(1)}, bf16[2,48,256]{2,1,0:T(8,128)(2,1)S(1)}, u32[]{:S(2)}, u32[]{:S(2)}) %collective-permute-start.4) | collective-permute-done | bytes 49184 | tf_op jit(solution)/shard_map/ppermute | solution.py:17
  90.2 3.6 %convolution_bitcast_fusion.1 = f32[2,8,32,4,32]{2,4,3,1,0:T(8,128)S(1)} fusion(bf16[2,8,128,4,32]{2,4,3,1,0:T(8,128)(2,1)S(1)} %bitcast.282, f32[2,8,4,32]{3,2,1,0:T(4,128)S(1)} %fusion.248, f32[2,8,4,32,128]{4,3,2,1,0:T(8,128)S(1)} %fusion.12), kind=kOutput, calls=%fused_computation.13 | convolution fusion | flops 17565824 | bytes 1843200 | tf_op jit(solution)/shard_map/swhqk,swkhd->swqhd/dot_general | solution.py:167
  95.2 1.2 fusion.249
  97.4 1.3 %fusion.91 = f32[2,256,512]{2,1,0:T(8,128)S(1)} fusion(f32[2,256,128]{1,2,0:T(8,128)S(1)} %get-tuple-element.75, bf16[3,128,512]{2,1,0:T(8,128)(2,1)} %param.28, f32[256,128]{0,1:T(8,128)S(1)} %copy-done.27, f32[2,256]{1,0:T(2,128)S(1)} %add_rsqrt_fusion.2, f32[2,256]{1,0:T(2,128)S(1)} %broadcast_multiply_fusion.3, f32[256,128]{0,1:T(8,128)S(1)} %copy-done.28), kind=kOutput, calls=%fused_computation.151 | convolution fusion | flops 67436544 | bytes 1708032 | tf_op jit(solution)/shard_map/sac,cf->saf/dot_general | solution.py:179
  100.9 1.2 fusion.251
  102.1 1.9 %collective-permute-start.7 = (bf16[2,48,256]{2,1,0:T(8,128)(2,1)S(1)}, bf16[2,48,256]{2,1,0:T(8,128)(2,1)S(1)}, u32[]{:S(2)}, u32[]{:S(2)}) collective-permute-start(bf16[2,48,256]{2,1,0:T(8,128)(2,1)S(1)} %get-tuple-element.33), channel_id=1, source_target_pairs={{8,0},{16,8},{24,16},{32,24},{40,32},{48,40},{56,48},{64,56},{72,6... | collective-permute-start | bytes 147464 | tf_op jit(solution)/shard_map/ppermute | solution.py:20
  104.0 2.4 %collective-permute-start.6 = (bf16[2,48,256]{2,1,0:T(8,128)(2,1)S(1)}, bf16[2,48,256]{2,1,0:T(8,128)(2,1)S(1)}, u32[]{:S(2)}, u32[]{:S(2)}) collective-permute-start(bf16[2,48,256]{2,1,0:T(8,128)(2,1)S(1)} %get-tuple-element.32), channel_id=1, source_target_pairs={{0,8},{8,16},{16,24},{24,32},{32,40},{40,48},{48,56},{56,64},{64,7... | collective-permute-start | bytes 147464 | tf_op jit(solution)/shard_map/ppermute | solution.py:17
  106.8 5.7 %collective-permute-done.6 = bf16[2,48,256]{2,1,0:T(8,128)(2,1)S(1)} collective-permute-done((bf16[2,48,256]{2,1,0:T(8,128)(2,1)S(1)}, bf16[2,48,256]{2,1,0:T(8,128)(2,1)S(1)}, u32[]{:S(2)}, u32[]{:S(2)}) %collective-permute-start.6) | collective-permute-done | bytes 49184 | tf_op jit(solution)/shard_map/ppermute | solution.py:17
  115.7 3.6 %convolution_bitcast_fusion = f32[2,8,32,4,32]{2,4,3,1,0:T(8,128)S(1)} fusion(bf16[2,8,128,4,32]{2,4,3,1,0:T(8,128)(2,1)S(1)} %bitcast.281, f32[2,8,4,32]{3,2,1,0:T(4,128)S(1)} %fusion.252, f32[2,8,4,32,128]{4,3,2,1,0:T(8,128)S(1)} %fusion.10), kind=kOutput, calls=%fused_computation.9 | convolution fusion | flops 17565824 | bytes 1843200 | tf_op jit(solution)/shard_map/swhqk,swkhd->swqhd/dot_general | solution.py:167
  120.7 1.2 fusion.253
  122.9 1.3 %fusion.93 = f32[2,256,512]{2,1,0:T(8,128)S(1)} fusion(f32[2,256,128]{1,2,0:T(8,128)S(1)} %get-tuple-element.81, bf16[3,128,512]{2,1,0:T(8,128)(2,1)} %param.28, f32[256,128]{0,1:T(8,128)S(1)} %copy-done.25, f32[2,256]{1,0:T(2,128)S(1)} %add_rsqrt_fusion, f32[2,256]{1,0:T(2,128)S(1)} %broadcast_multiply_fusion.1, f32[256,128]{0,1:T(8,128)S(1)} %copy-done.26), kind=kOutput, calls=%fused_computation.153 | convolution fusion | flops 67436544 | bytes 1708032 | tf_op jit(solution)/shard_map/sac,cf->saf/dot_general | solution.py:179
  (236 shorter events, 56.3 us)
Async XLA Ops:
  0.0 30.6 %copy-start = (f32[16,9]{1,0:T(8,128)S(1)}, f32[16,9]{1,0:T(8,128)}, u32[]{:S(2)}) copy-start(f32[16,9]{1,0:T(8,128)} %param.20) | copy-start | bytes 1732
  0.0 1.0 copy-start.2
  3.4 22.4 %copy-start.5 = (bf16[3,128,768]{2,1,0:T(8,128)(2,1)S(1)}, bf16[3,128,768]{2,1,0:T(8,128)(2,1)}, u32[]{:S(2)}) copy-start(bf16[3,128,768]{2,1,0:T(8,128)(2,1)} %param.24) | copy-start | bytes 1769476
  5.6 10.4 %copy-start.40 = (bf16[2,128,16]{1,2,0:T(8,128)(2,1)S(1)}, bf16[2,128,16]{1,2,0:T(8,128)(2,1)}, u32[]{:S(2)}) copy-start(bf16[2,128,16]{1,2,0:T(8,128)(2,1)} %param.21) | copy-start | bytes 24580
  6.3 51.0 %collective-permute-start.1 = (bf16[2,48,256]{2,1,0:T(8,128)(2,1)}, bf16[2,48,256]{2,1,0:T(8,128)(2,1)S(1)}, u32[]{:S(2)}, u32[]{:S(2)}) collective-permute-start(bf16[2,48,256]{2,1,0:T(8,128)(2,1)} %get-tuple-element.37), channel_id=1, source_target_pairs={{8,0},{16,8},{24,16},{32,24},{40,32},{48,40},{56,48},{64,56},{72,6... | collective-permute-start | bytes 147464 | tf_op jit(solution)/shard_map/ppermute | solution.py:20
  14.1 2.1 %copy-start.44 = (s32[256]{0:T(256)S(1)}, s32[256]{0:T(256)}, u32[]{:S(2)}) copy-start(s32[256]{0:T(256)} %param.18) | copy-start | bytes 3076
  14.1 43.2 %collective-permute-start = (bf16[2,48,256]{2,1,0:T(8,128)(2,1)}, bf16[2,48,256]{2,1,0:T(8,128)(2,1)}, u32[]{:S(2)}, u32[]{:S(2)}) collective-permute-start(bf16[2,48,256]{2,1,0:T(8,128)(2,1)} %get-tuple-element.36), channel_id=1, source_target_pairs={{0,8},{8,16},{16,24},{24,32},{32,40},{40,48},{48,56},{56,64},{64,7... | collective-permute-start | bytes 147464 | tf_op jit(solution)/shard_map/ppermute | solution.py:17
  16.9 12.5 %collective-permute-start.2 = (f32[20,48]{1,0:T(8,128)S(1)}, f32[20,48]{1,0:T(8,128)S(1)}, u32[]{:S(2)}, u32[]{:S(2)}) collective-permute-start(f32[20,48]{1,0:T(8,128)S(1)} %get-tuple-element.55), channel_id=1, source_target_pairs={{0,8},{8,16},{16,24},{24,32},{32,40},{40,48},{48,56},{56,64},{64,7... | collective-permute-start | bytes 11528 | tf_op jit(solution)/shard_map/ppermute | solution.py:17
  18.8 10.6 %collective-permute-start.3 = (f32[20,48]{1,0:T(8,128)S(1)}, f32[20,48]{1,0:T(8,128)S(1)}, u32[]{:S(2)}, u32[]{:S(2)}) collective-permute-start(f32[20,48]{1,0:T(8,128)S(1)} %get-tuple-element.54), channel_id=1, source_target_pairs={{8,0},{16,8},{24,16},{32,24},{40,32},{48,40},{56,48},{64,56},{72,6... | collective-permute-start | bytes 11528 | tf_op jit(solution)/shard_map/ppermute | solution.py:20
  26.4 1.5 %copy-start.37 = (f32[20,1,32]{2,1,0:T(1,128)}, f32[20,1,32]{2,1,0:T(1,128)S(1)}, u32[]{:S(2)}) copy-start(f32[20,1,32]{2,1,0:T(1,128)S(1)} %fusion.202) | copy-start | bytes 7684
  34.8 5.4 %copy-start.43 = (f32[3,128]{1,0:T(4,128)S(1)}, f32[3,128]{1,0:T(4,128)}, u32[]{:S(2)}) copy-start(f32[3,128]{1,0:T(4,128)} %param.26) | copy-start | bytes 4612
  34.8 25.2 %all-to-all-start = ((bf16[8,3,1,4,32,128]{5,4,3,2,1,0:T(8,128)(2,1)}), bf16[8,3,1,4,32,128]{5,4,3,2,1,0:T(8,128)(2,1)S(1)}, u32[]{:S(2)}, u32[]{:S(2)}) async-start(bf16[8,3,1,4,32,128]{5,4,3,2,1,0:T(8,128)(2,1)} %stack.81), calls=%async_computation | async-start | bytes 1572864 | tf_op jit(solution)/shard_map/all_to_all | solution.py:130
  61.3 1.0 copy-start.22
  69.5 1.3 %copy-start.35 = (f32[256,128]{0,1:T(8,128)S(1)}, f32[256,128]{0,1:T(8,128)}, u32[]{:S(2)}) copy-start(f32[256,128]{0,1:T(8,128)} %copy.197) | copy-start | bytes 393220
  74.2 12.1 %copy-start.4 = (f32[2,256,512]{2,1,0:T(8,128)}, f32[2,256,512]{2,1,0:T(8,128)S(1)}, u32[]{:S(2)}) copy-start(f32[2,256,512]{2,1,0:T(8,128)S(1)} %get-tuple-element.73) | copy-start | bytes 3145732
  74.2 6.6 %collective-permute-start.5 = (bf16[2,48,256]{2,1,0:T(8,128)(2,1)S(1)}, bf16[2,48,256]{2,1,0:T(8,128)(2,1)S(1)}, u32[]{:S(2)}, u32[]{:S(2)}) collective-permute-start(bf16[2,48,256]{2,1,0:T(8,128)(2,1)S(1)} %get-tuple-element.35), channel_id=1, source_target_pairs={{8,0},{16,8},{24,16},{32,24},{40,32},{48,40},{56,48},{64,56},{72,6... | collective-permute-start | bytes 147464 | tf_op jit(solution)/shard_map/ppermute | solution.py:20
  77.7 8.5 %collective-permute-start.4 = (bf16[2,48,256]{2,1,0:T(8,128)(2,1)S(1)}, bf16[2,48,256]{2,1,0:T(8,128)(2,1)S(1)}, u32[]{:S(2)}, u32[]{:S(2)}) collective-permute-start(bf16[2,48,256]{2,1,0:T(8,128)(2,1)S(1)} %get-tuple-element.34), channel_id=1, source_target_pairs={{0,8},{8,16},{16,24},{24,32},{32,40},{40,48},{48,56},{56,64},{64,7... | collective-permute-start | bytes 147464 | tf_op jit(solution)/shard_map/ppermute | solution.py:17
  89.2 1.0 copy-start.24
  97.4 1.3 %copy-start.33 = (f32[256,128]{0,1:T(8,128)S(1)}, f32[256,128]{0,1:T(8,128)}, u32[]{:S(2)}) copy-start(f32[256,128]{0,1:T(8,128)} %copy.214) | copy-start | bytes 393220
  102.1 10.4 %copy-start.3 = (f32[2,256,512]{2,1,0:T(8,128)}, f32[2,256,512]{2,1,0:T(8,128)S(1)}, u32[]{:S(2)}) copy-start(f32[2,256,512]{2,1,0:T(8,128)S(1)} %get-tuple-element.79) | copy-start | bytes 3145732
  102.1 4.7 %collective-permute-start.7 = (bf16[2,48,256]{2,1,0:T(8,128)(2,1)S(1)}, bf16[2,48,256]{2,1,0:T(8,128)(2,1)S(1)}, u32[]{:S(2)}, u32[]{:S(2)}) collective-permute-start(bf16[2,48,256]{2,1,0:T(8,128)(2,1)S(1)} %get-tuple-element.33), channel_id=1, source_target_pairs={{8,0},{16,8},{24,16},{32,24},{40,32},{48,40},{56,48},{64,56},{72,6... | collective-permute-start | bytes 147464 | tf_op jit(solution)/shard_map/ppermute | solution.py:20
  104.0 8.4 %collective-permute-start.6 = (bf16[2,48,256]{2,1,0:T(8,128)(2,1)S(1)}, bf16[2,48,256]{2,1,0:T(8,128)(2,1)S(1)}, u32[]{:S(2)}, u32[]{:S(2)}) collective-permute-start(bf16[2,48,256]{2,1,0:T(8,128)(2,1)S(1)} %get-tuple-element.32), channel_id=1, source_target_pairs={{0,8},{8,16},{16,24},{24,32},{32,40},{40,48},{48,56},{56,64},{64,7... | collective-permute-start | bytes 147464 | tf_op jit(solution)/shard_map/ppermute | solution.py:17
  114.7 1.0 copy-start.23
  122.9 1.3 %copy-start.31 = (f32[256,128]{0,1:T(8,128)S(1)}, f32[256,128]{0,1:T(8,128)}, u32[]{:S(2)}) copy-start(f32[256,128]{0,1:T(8,128)} %copy.231) | copy-start | bytes 393220
  (34 other events, 29.7 us)
